TPU v7x, 32 devices: a whole 2x2x4 slice. The times are simulated.
32 devices in a mesh: groups: 2 (over y), section: 4 (over z), tp: 2 (over core), sp: 2 (over x).
Axes of the slice: x: 2, y: 2, z: 4, core: 2. Of those that a mesh axis runs over, the one named last changes fastest.
Arguments:
- hidden: bfloat16 [1024, 6144], P(('groups', 'sp', 'section'), 'tp'), parts along dimension 0, may hold values from -6 to 6
- modulation: float32 [2, 6144], P(None, 'tp'), may hold values from -2 to 2
- time_embed: float32 [12288], P(('groups', 'tp')), parts along dimension 0, may hold values from -2 to 2
- head_weight: bfloat16 [6144, 64], P('tp'), may hold values from -0.078125 to 0.078125
- head_bias: float32 [64], replicated, may hold values from -2 to 2
- noisy: bfloat16 [16, 16, 16, 16], P(('groups', 'sp'), None, 'section'), parts along dimension 0, may hold values from -6 to 6
- step_size: float32 [2], P('groups'), parts along dimension 0, may hold values from 0.2 to 0.6
- latent_mean: float32 [16], replicated, may hold values from -2 to 2
- latent_std: float32 [16], replicated, may hold values from 0.5 to 2
- in_weight: bfloat16 [27, 16, 512], P(None, None, 'tp'), may hold values from -0.3125 to 0.3125
- in_bias: float32 [512], P('tp'), may hold values from -2 to 2
- norm_gain: float32 [512], replicated, may hold values from 0.25 to 1.75
- conv_weight: bfloat16 [27, 512, 512], P(None, 'section', 'tp'), may hold values from -0.0546875 to 0.0546875
- conv_bias: float32 [512], P('tp'), may hold values from -2 to 2
Outputs:
- decoded: bfloat16 [16, 16, 16, 512], P(('groups', 'sp'), None, 'section', 'tp'), parts along dimension 0
There are 2 independent parts, one for each index of `groups`. A program takes and returns all parts, laid end to end along the dimension named above; an argument that names none is the same for every part. Nothing has to cross between parts.
All inputs are finite; a program needn't handle non-finite values.
Results may differ from a plain program's by a relative error of at most 0.006.
Values may be sent and summed in bfloat16 or wider, within the bound.
No kernel may reach another device: no remote copies, remote signals or barrier semaphores. Data moves between devices by JAX's collectives and lax.ppermute only.
A program may use at most 128 MiB of HBM per device.

v0:
```python
import jax
import jax.numpy as jnp
from jax import lax
from jax.sharding import PartitionSpec as P

D = 6144


def padded_2(value, sides, width):
    for axis, dim in sides:
        count, length = (lax.axis_size(axis), value.shape[dim])
        up = [(i, (i + 1) % count) for i in range(count - 1)]
        down = [(j, i) for i, j in up]
        last = lax.slice_in_dim(value, length - width, length, axis=dim)
        leading = lax.slice_in_dim(value, 0, width, axis=dim)
        before = lax.ppermute(last, axis, up)
        after = lax.ppermute(leading, axis, down)
        value = jnp.concatenate([before, value, after], axis=dim)
    return value


def passed_along(value, axis, by):
    count = lax.axis_size(axis)
    pairs = [(i, i + by) for i in range(count) if 0 <= i + by < count]
    return lax.ppermute(value, axis, pairs)


def conv_taps(padded, weight, frames, height, columns):
    channels = padded.shape[3]
    result = jnp.zeros((frames * height * columns, weight.shape[2]), jnp.float32)
    for offset_time in range(3):
        for offset_row in range(3):
            slab = padded[offset_time : offset_time + frames, offset_row : offset_row + height]
            window = jnp.concatenate(
                [slab[:, :, 0:columns], slab[:, :, 1 : columns + 1], slab[:, :, 2 : columns + 2]],
                axis=3,
            )
            first = 9 * offset_time + 3 * offset_row
            taps = weight[first : first + 3].reshape(3 * channels, weight.shape[2])
            result = result + jnp.dot(
                window.reshape(-1, 3 * channels), taps, preferred_element_type=jnp.float32
            )
    return result


def activate(source, gain_vector):
    values = source.astype(jnp.float32)
    squares = jnp.mean(values * values, axis=-1, keepdims=True)
    return jax.nn.silu(values * lax.rsqrt(squares + 1e-06) * gain_vector).astype(jnp.bfloat16)


def pad_rows(source):
    return jnp.pad(source, ((0, 0), (1, 1), (0, 0), (0, 0)))


def shards(
    hidden,
    modulation,
    time_embed,
    head_weight,
    head_bias,
    noisy,
    step_size,
    latent_mean,
    latent_std,
    in_weight,
    in_bias,
    norm_gain,
    conv_weight,
    conv_bias,
):
    frames, height, columns, lat_channels = noisy.shape
    sections = lax.axis_size("section")
    half_channels = in_weight.shape[2]
    values = hidden.astype(jnp.float32)
    row_sums, square_sums = lax.psum(
        (jnp.sum(values, axis=1), jnp.sum(values * values, axis=1)), "tp"
    )
    average = row_sums / D
    variance = square_sums / D - average * average
    shift_term = modulation[0] + time_embed
    scale_term = modulation[1] + time_embed
    modulated = (
        (values - average[:, None]) * lax.rsqrt(variance[:, None] + 1e-06) * (1.0 + scale_term)
        + shift_term
    ).astype(jnp.bfloat16)
    partial_sum = jnp.dot(modulated, head_weight, preferred_element_type=jnp.float32)
    velocity = (lax.psum(partial_sum, "tp") + head_bias).astype(jnp.bfloat16)
    band_rows = velocity.shape[0] * 2 // (columns * sections)
    outgoing = velocity.reshape(band_rows, sections, -1)
    arrived = lax.all_to_all(outgoing, "section", split_axis=1, concat_axis=0, tiled=True)
    latent_field = arrived.reshape(frames, height // 2, columns // 2, 2, 2, lat_channels)
    latent_field = jnp.transpose(latent_field, (0, 1, 3, 2, 4, 5)).reshape(
        frames, height, columns, lat_channels
    )
    latent = (
        (noisy.astype(jnp.float32) - step_size[0] * latent_field.astype(jnp.float32)) * latent_std
        + latent_mean
    ).astype(jnp.bfloat16)
    latent_wide = padded_2(latent, (("section", 2),), 2)
    earlier = passed_along(latent_wide, "sp", 1)
    stacked = pad_rows(jnp.concatenate([earlier, latent_wide], axis=0))
    extended = (conv_taps(stacked, in_weight, frames + 2, height, columns + 2) + in_bias).astype(
        jnp.bfloat16
    )
    extended = extended.reshape(frames + 2, height, columns + 2, half_channels)
    upblock_half = extended[2:, :, 1 : columns + 1]
    extended_full = lax.all_gather(extended, "tp", axis=3, tiled=True)
    normed = activate(extended_full, norm_gain)
    frame_index = lax.axis_index("sp") * frames - 2 + jnp.arange(frames + 2, dtype=jnp.int32)
    column_index = (
        lax.axis_index("section") * columns - 1 + jnp.arange(columns + 2, dtype=jnp.int32)
    )
    inside_cols = (column_index >= 0) & (column_index < columns * sections)
    inside = (frame_index >= 0)[:, None, None, None] & inside_cols[None, None, :, None]
    conv_input = pad_rows(jnp.where(inside, normed, jnp.zeros_like(normed)))
    full_weight = lax.all_gather(conv_weight, "section", axis=1, tiled=True)
    mixed = conv_taps(conv_input, full_weight, frames, height, columns)
    decoded = (
        upblock_half.astype(jnp.float32).reshape(-1, half_channels) + mixed + conv_bias
    ).astype(jnp.bfloat16)
    return decoded.reshape(frames, height, columns, half_channels)


def solution(mesh):
    placed = (
        P(("groups", "sp", "section"), "tp"),
        P(None, "tp"),
        P(("groups", "tp")),
        P("tp", None),
        P(),
        P(("groups", "sp"), None, "section", None),
        P("groups"),
        P(),
        P(),
        P(None, None, "tp"),
        P("tp"),
        P(),
        P(None, "section", "tp"),
        P("tp"),
    )
    return jax.shard_map(
        shards,
        mesh=mesh,
        in_specs=placed,
        out_specs=P(("groups", "sp"), None, "section", "tp"),
        check_vma=False,
    )
```

profile of v0, /device:TPU:0, one launch (start us, length us, event | category | flops | bytes accessed | tf_op | source)
XLA Modules:
  0.0 158.0 jit_solution(14631500808163563009)
XLA Ops:
  6.6 0.7 all-gather.2.cloned.1.call-update
  7.8 2.6 %all-reduce.2 = (f32[64]{0:T(128)S(1)}, f32[64]{0:T(128)S(1)}) all-reduce(f32[64]{0:T(128)S(1)} %get-tuple-element.6, f32[64]{0:T(128)S(1)} %get-tuple-element.5), channel_id=1, replica_groups=mesh['groups'=2,'section'=4,'tp'=2,'sp'=2] {'tp'}, use_global_device_ids=true, to_apply=%region_3.0 | all-reduce | flops 128 | bytes 1024 | tf_op jit(solution)/shard_map/psum | solution.py:76
  10.8 3.6 %psum.23 = f32[64,64]{1,0:T(8,128)S(1)} all-reduce(f32[64,64]{1,0:T(8,128)S(1)} %fusion.19), channel_id=1, replica_groups=mesh['groups'=2,'section'=4,'tp'=2,'sp'=2] {'tp'}, use_global_device_ids=true, to_apply=%region_4.0 | all-reduce | flops 4096 | bytes 32768 | tf_op jit(solution)/shard_map/psum | solution.py:88
  14.5 0.6 copy.17
  15.1 6.0 %all-to-all-start = ((bf16[8,4,128]{2,0,1:T(8,128)(2,1)}), bf16[8,4,128]{2,0,1:T(8,128)(2,1)S(1)}, u32[]{:S(2)}, u32[]{:S(2)}) async-start(bf16[8,4,128]{2,0,1:T(8,128)(2,1)} %copy.17), calls=%async_computation | async-start | bytes 16384 | tf_op jit(solution)/shard_map/all_to_all | solution.py:91
  21.2 0.7 fusion.28
  22.5 7.5 %all-to-all-done = bf16[8,4,128]{2,0,1:T(8,128)(2,1)S(1)} async-done(((bf16[8,4,128]{2,0,1:T(8,128)(2,1)}), bf16[8,4,128]{2,0,1:T(8,128)(2,1)S(1)}, u32[]{:S(2)}, u32[]{:S(2)}) %all-to-all-start) | async-done | bytes 8224 | tf_op jit(solution)/shard_map/all_to_all | solution.py:91
  30.4 1.3 collective-permute-start
  31.7 1.3 collective-permute-start.1
  33.0 0.9 collective-permute-done
  33.9 4.4 %collective-permute-done.1 = bf16[4,16,2,16]{3,2,1,0:T(2,128)(2,1)S(1)} collective-permute-done((bf16[4,16,2,16]{3,2,1,0:T(2,128)(2,1)S(1)}, bf16[4,16,2,16]{3,2,1,0:T(2,128)(2,1)S(1)}, u32[]{:S(2)}, u32[]{:S(2)}) %collective-permute-start.1) | collective-permute-done | bytes 4128 | tf_op jit(solution)/shard_map/ppermute | solution.py:17
  38.5 3.4 %collective-permute-start.2 = (bf16[4,16,8,16]{3,2,1,0:T(8,128)(2,1)S(1)}, bf16[4,16,8,16]{3,2,1,0:T(8,128)(2,1)S(1)}, u32[]{:S(2)}, u32[]{:S(2)}) collective-permute-start(bf16[4,16,8,16]{3,2,1,0:T(8,128)(2,1)S(1)} %pad_maximum_fusion.18), channel_id=1, source_target_pairs={{0,1},{2,3},{4,5},{6,7},{8,9},{10,11},{12,13},{14,15},{16,17},{18,... | collective-permute-start | bytes 49160 | tf_op jit(solution)/shard_map/ppermute | solution.py:25
  41.9 0.6 broadcast_and_fusion
  42.5 1.9 %collective-permute-done.2 = bf16[4,16,8,16]{3,2,1,0:T(8,128)(2,1)S(1)} collective-permute-done((bf16[4,16,8,16]{3,2,1,0:T(8,128)(2,1)S(1)}, bf16[4,16,8,16]{3,2,1,0:T(8,128)(2,1)S(1)}, u32[]{:S(2)}, u32[]{:S(2)}) %collective-permute-start.2) | collective-permute-done | bytes 16416 | tf_op jit(solution)/shard_map/ppermute | solution.py:25
  44.8 1.0 pad_slice_fusion.2
  45.8 0.4 pad_maximum_fusion.9
  46.2 0.8 reshape.198
  47.1 1.3 pad_slice_fusion.1
  48.3 1.1 pad_maximum_fusion.10
  49.4 0.7 reshape.200
  50.2 2.2 %pad_maximum_fusion.12 = (bf16[6,16,6,48]{3,2,1,0:T(8,128)(2,1)}, bf16[6,16,6,48]{3,2,1,0:T(8,128)(2,1)S(1)}) fusion(bf16[6,16,6,16]{3,2,1,0:T(8,128)(2,1)S(1)} %get-tuple-element.53, bf16[6,16,6,16]{3,2,1,0:T(8,128)(2,1)S(1)} %get-tuple-element.52, bf16[6,16,6,16]{3,2,1,0:T(8,128)(2,1)S(1)} %get-tuple-element.51, ...), kind=kLoop, calls=%fused_computation.58 | loop fusion | flops 331776 | bytes 221184 | tf_op jit(solution)/shard_map/concatenate | solution.py:34
  52.4 1.7 %reshape.204 = bf16[576,48]{1,0:T(8,128)(2,1)} reshape(bf16[6,16,6,48]{3,2,1,0:T(8,128)(2,1)} %get-tuple-element.91) | data formatting | bytes 110592 | tf_op jit(solution)/shard_map/reshape | solution.py:41
  54.6 0.4 pad_maximum_fusion.14
  58.2 0.8 reshape.239
  59.0 2.5 %all_gather.6 = bf16[6,16,6,512]{3,2,1,0:T(8,128)(2,1)S(1)} all-gather(bf16[6,16,6,256]{3,2,1,0:T(8,128)(2,1)S(1)} %reshape.216), channel_id=1, replica_groups=mesh['groups'=2,'section'=4,'tp'=2,'sp'=2] {'tp'}, dimensions={3}, use_global_device_ids=true | all-gather | bytes 884736 | tf_op jit(solution)/shard_map/all_gather | solution.py:108
  61.8 0.6 fusion.18
  62.4 1.4 fusion.26
  64.3 2.3 %pad_slice_fusion.20 = (bf16[4,16,4,512]{3,2,1,0:T(4,128)(2,1)}, bf16[4,16,4,512]{3,2,1,0:T(4,128)(2,1)S(1)}, bf16[4,16,4,512]{3,2,1,0:T(4,128)(2,1)S(1)}, bf16[...) fusion(bf16[6,16,6,512]{3,2,1,0:T(8,128)(2,1)S(1)} %fusion.18), kind=kLoop, calls=%fused_computation.96 | loop fusion | bytes 3670016 | tf_op jit(solution)/shard_map/slice | solution.py:35
  67.2 1.5 pad_maximum_fusion.2
  68.6 1.1 reshape.223
  69.8 1.5 pad_maximum_fusion.3
  71.2 1.1 reshape.225
  72.4 2.5 %pad_slice_fusion.19 = (bf16[4,16,4,512]{3,2,1,0:T(4,128)(2,1)S(1)}, bf16[4,16,4,512]{3,2,1,0:T(4,128)(2,1)}, bf16[4,16,4,512]{3,2,1,0:T(4,128)(2,1)}, bf16[4,16...) fusion(bf16[6,16,6,512]{3,2,1,0:T(8,128)(2,1)S(1)} %fusion.18), kind=kLoop, calls=%fused_computation.95 | loop fusion | bytes 4456448 | tf_op jit(solution)/shard_map/slice | solution.py:35
  75.4 1.5 pad_maximum_fusion.4
  76.8 1.1 reshape.227
  77.9 1.5 pad_maximum_fusion.7
  79.4 1.1 reshape.233
  80.4 1.4 pad_maximum_fusion.5
  81.9 1.1 reshape.229
  82.9 1.4 pad_maximum_fusion.6
  84.4 1.1 reshape.231
  85.5 55.2 %all-gather.2.cloned.1.call-done = bf16[27,512,256]{2,1,0:T(8,128)(2,1)} async-done(((bf16[27,128,256]{2,1,0:T(8,128)(2,1)}), bf16[27,512,256]{2,1,0:T(8,128)(2,1)}) %all-gather.2.cloned.1.call-update) | async-done | bytes 7077904 | tf_op jit(solution)/shard_map/all_gather | solution.py:117
  140.7 3.8 %fusion.25 = (bf16[3,512,256]{2,1,0:T(8,128)(2,1)S(1)}, bf16[3,512,256]{2,1,0:T(8,128)(2,1)S(1)}, bf16[3,512,256]{2,1,0:T(8,128)(2,1)S(1)}, bf16[3,512,256]{2,1,...) fusion(bf16[27,512,256]{2,1,0:T(8,128)(2,1)} %all-gather.2.clon, ...), kind=kLoop, calls=%fused_computation.112 | loop fusion | bytes 14155776 | tf_op jit(solution)/shard_map/slice | solution.py:39
  146.0 0.4 copy-done.2
  147.5 0.4 copy-done.5
  149.1 0.4 copy-done.3
  150.1 0.4 fusion.12
  150.5 0.7 reshape.237
  (126 shorter events, 11.5 us)
Async XLA Ops:
  6.5 3.9 %copy-start = (bf16[3072,64]{0,1:T(8,128)(2,1)S(1)}, bf16[3072,64]{0,1:T(8,128)(2,1)}, u32[]{:S(2)}) copy-start(bf16[3072,64]{0,1:T(8,128)(2,1)} %param.17) | copy-start | bytes 1179652
  6.5 0.8 copy-start.30
  6.5 1.1 copy-start.18
  6.5 3.9 %copy-start.31 = (f32[3072]{0:T(1024)S(1)}, f32[3072]{0:T(1024)}, u32[]{:S(2)}) copy-start(f32[3072]{0:T(1024)} %param.16) | copy-start | bytes 36868
  6.5 7.9 %copy-start.36 = (f32[64]{0:T(128)S(1)}, f32[64]{0:T(128)}, u32[]{:S(2)}) copy-start(f32[64]{0:T(128)} %param.18) | copy-start | bytes 772
  6.5 14.6 %copy-start.19 = (bf16[27,16,256]{2,1,0:T(8,128)(2,1)S(1)}, bf16[27,16,256]{2,1,0:T(8,128)(2,1)}, u32[]{:S(2)}) copy-start(bf16[27,16,256]{2,1,0:T(8,128)(2,1)} %param.23) | copy-start | bytes 663556
  6.6 134.1 %all-gather.2.cloned.1.call-start = ((), (), s32[]{:S(2)}) async-start(), calls=%async_computation.1 | async-start | bytes 8847360 | tf_op jit(solution)/shard_map/all_gather | solution.py:117
  7.3 22.9 %copy-start.29 = (bf16[4,16,4,16]{3,2,1,0:T(4,128)(2,1)S(1)}, bf16[4,16,4,16]{3,2,1,0:T(4,128)(2,1)}, u32[]{:S(2)}) copy-start(bf16[4,16,4,16]{3,2,1,0:T(4,128)(2,1)} %param.19) | copy-start | bytes 24580
  7.3 22.9 %copy-start.37 = (f32[16]{0:T(128)S(1)}, f32[16]{0:T(128)}, u32[]{:S(2)}) copy-start(f32[16]{0:T(128)} %param.21) | copy-start | bytes 196
  7.3 23.0 %copy-start.38 = (f32[16]{0:T(128)S(1)}, f32[16]{0:T(128)}, u32[]{:S(2)}) copy-start(f32[16]{0:T(128)} %param.22) | copy-start | bytes 196
  15.1 14.9 %all-to-all-start = ((bf16[8,4,128]{2,0,1:T(8,128)(2,1)}), bf16[8,4,128]{2,0,1:T(8,128)(2,1)S(1)}, u32[]{:S(2)}, u32[]{:S(2)}) async-start(bf16[8,4,128]{2,0,1:T(8,128)(2,1)} %copy.17), calls=%async_computation | async-start | bytes 16384 | tf_op jit(solution)/shard_map/all_to_all | solution.py:91
  30.4 3.5 %collective-permute-start = (bf16[4,16,2,16]{3,2,1,0:T(2,128)(2,1)S(1)}, bf16[4,16,2,16]{3,2,1,0:T(2,128)(2,1)S(1)}, u32[]{:S(2)}, u32[]{:S(2)}) collective-permute-start(bf16[4,16,2,16]{3,2,1,0:T(2,128)(2,1)S(1)} %get-tuple-element.81), channel_id=1, source_target_pairs={{0,4},{4,8},{8,12},{1,5},{5,9},{9,13},{2,6},{6,10},{10,14},{3,7},{... | collective-permute-start | bytes 12296 | tf_op jit(solution)/shard_map/ppermute | solution.py:16
  31.7 6.6 %collective-permute-start.1 = (bf16[4,16,2,16]{3,2,1,0:T(2,128)(2,1)S(1)}, bf16[4,16,2,16]{3,2,1,0:T(2,128)(2,1)S(1)}, u32[]{:S(2)}, u32[]{:S(2)}) collective-permute-start(bf16[4,16,2,16]{3,2,1,0:T(2,128)(2,1)S(1)} %get-tuple-element.82), channel_id=1, source_target_pairs={{4,0},{8,4},{12,8},{5,1},{9,5},{13,9},{6,2},{10,6},{14,10},{7,3},{... | collective-permute-start | bytes 12296 | tf_op jit(solution)/shard_map/ppermute | solution.py:17
  38.5 5.9 %collective-permute-start.2 = (bf16[4,16,8,16]{3,2,1,0:T(8,128)(2,1)S(1)}, bf16[4,16,8,16]{3,2,1,0:T(8,128)(2,1)S(1)}, u32[]{:S(2)}, u32[]{:S(2)}) collective-permute-start(bf16[4,16,8,16]{3,2,1,0:T(8,128)(2,1)S(1)} %pad_maximum_fusion.18), channel_id=1, source_target_pairs={{0,1},{2,3},{4,5},{6,7},{8,9},{10,11},{12,13},{14,15},{16,17},{18,... | collective-permute-start | bytes 49160 | tf_op jit(solution)/shard_map/ppermute | solution.py:25
  49.4 4.6 %copy-start.11 = (bf16[6,16,6,16]{3,2,1,0:T(8,128)(2,1)S(1)}, bf16[6,16,6,16]{3,2,1,0:T(8,128)(2,1)}, u32[]{:S(2)}) copy-start(bf16[6,16,6,16]{3,2,1,0:T(8,128)(2,1)} %get-tuple-element.45) | copy-start | bytes 55300
  49.4 4.6 %copy-start.12 = (bf16[6,16,6,16]{3,2,1,0:T(8,128)(2,1)S(1)}, bf16[6,16,6,16]{3,2,1,0:T(8,128)(2,1)}, u32[]{:S(2)}) copy-start(bf16[6,16,6,16]{3,2,1,0:T(8,128)(2,1)} %get-tuple-element.55) | copy-start | bytes 55300
  49.4 4.6 %copy-start.13 = (bf16[6,16,6,16]{3,2,1,0:T(8,128)(2,1)S(1)}, bf16[6,16,6,16]{3,2,1,0:T(8,128)(2,1)}, u32[]{:S(2)}) copy-start(bf16[6,16,6,16]{3,2,1,0:T(8,128)(2,1)} %get-tuple-element.62) | copy-start | bytes 55300
  50.2 4.3 %copy-start.14 = (bf16[6,16,6,48]{3,2,1,0:T(8,128)(2,1)S(1)}, bf16[6,16,6,48]{3,2,1,0:T(8,128)(2,1)}, u32[]{:S(2)}) copy-start(bf16[6,16,6,48]{3,2,1,0:T(8,128)(2,1)} %get-tuple-element.94) | copy-start | bytes 165892
  50.2 4.4 %copy-start.10 = (bf16[6,16,6,16]{3,2,1,0:T(8,128)(2,1)S(1)}, bf16[6,16,6,16]{3,2,1,0:T(8,128)(2,1)}, u32[]{:S(2)}) copy-start(bf16[6,16,6,16]{3,2,1,0:T(8,128)(2,1)} %get-tuple-element.61) | copy-start | bytes 55300
  54.3 1.0 copy-start.15
  54.3 1.0 copy-start.20
  54.6 0.9 copy-start.16
  54.6 0.9 copy-start.28
  55.0 0.8 copy-start.27
  55.2 0.9 copy-start.17
  55.3 0.9 copy-start.26
  55.7 0.8 copy-start.25
  56.0 0.8 copy-start.24
  56.4 0.7 copy-start.23
  56.7 0.7 copy-start.22
  57.0 0.7 copy-start.21
  57.0 0.7 copy-start.34
  58.1 3.7 %copy-start.32 = (pred[6,6]{1,0:T(8,128)(4,1)S(1)}, pred[6,6]{1,0:T(8,128)(4,1)}, u32[]{:S(2)}) copy-start(pred[6,6]{1,0:T(8,128)(4,1)} %broadcast_and_fusion) | copy-start | bytes 112
  58.1 3.7 %copy-start.33 = (f32[512]{0:T(512)S(1)}, f32[512]{0:T(512)}, u32[]{:S(2)}) copy-start(f32[512]{0:T(512)} %param.25) | copy-start | bytes 6148
  64.3 2.3 %copy-start.8 = (bf16[4,16,4,512]{3,2,1,0:T(4,128)(2,1)S(1)}, bf16[4,16,4,512]{3,2,1,0:T(4,128)(2,1)}, u32[]{:S(2)}) copy-start(bf16[4,16,4,512]{3,2,1,0:T(4,128)(2,1)} %get-tuple-element.44) | copy-start | bytes 786436
  72.4 2.5 %copy-start.7 = (bf16[4,16,4,512]{3,2,1,0:T(4,128)(2,1)S(1)}, bf16[4,16,4,512]{3,2,1,0:T(4,128)(2,1)}, u32[]{:S(2)}) copy-start(bf16[4,16,4,512]{3,2,1,0:T(4,128)(2,1)} %get-tuple-element.18) | copy-start | bytes 786436
  144.4 1.1 copy-start.1
  145.2 1.2 copy-start.2
  146.0 1.2 copy-start.4
  146.8 1.2 copy-start.5
  147.5 1.2 copy-start.6
  148.3 1.2 copy-start.3
  149.1 1.0 copy-start.9
  149.1 1.0 copy-start.35
Sparse Core Ops, SparseCore 0:
  8.9 131.6 all-gather.1
where the time goes:
time: 159 us; the launch traced here: 158 us
  waiting for transfers between devices  70.6 us (44%)
  local copies, waits for them, and re-layouts  30.1 us (19%)
  other arithmetic  16.3 us (10%)
  between operations  14.7 us (9%)
  starting transfers between devices  12 us (8%)
  blocking collectives  8.74 us (5%)
  matrix products  5.53 us (3%)
    all_gather x1, waiting for transfers between devices, shards(): full_weight = lax.all_gather(conv_weight, 'section', axis=1, tiled=True)  55.2 us
    concatenate x14, other arithmetic, conv_taps(): jnp.concatenate([slab[:, :, 0:columns], slab[:, :, 1:columns + 1], slab[:...  14.1 us
    reshape x18, local copies, waits for them, and re-layouts, conv_taps(): window.reshape(-1, 3 * channels)  10.7 us
    all_to_all x1, waiting for transfers between devices, shards(): lax.all_to_all(outgoing, 'section', split_axis=1, concat_axis=0, tiled=True)  7.51 us
    all_to_all x1, starting transfers between devices, shards(): lax.all_to_all(outgoing, 'section', split_axis=1, concat_axis=0, tiled=True)  6.02 us
    dot_general x18, matrix products, conv_taps(): jnp.dot(window.reshape(-1, 3 * channels), taps, preferred_element_type=jn...  5.17 us
    slice x4, local copies, waits for them, and re-layouts, conv_taps(): slab[:, :, 0:columns]  4.94 us
    slice x2, local copies, waits for them, and re-layouts, conv_taps(): taps = weight[first:first + 3].reshape(3 * channels, weight.shape[2])  4.44 us
  transfers between devices with their start and end apart: 5, of which 5 were waited for; matrix products, arithmetic and copies ran while one was open for 26% of the time, Pallas kernels for 0%

commit v1 on v0

--- a/solution.py
+++ b/solution.py
@@ -114,7 +114,21 @@
     inside_cols = (column_index >= 0) & (column_index < columns * sections)
     inside = (frame_index >= 0)[:, None, None, None] & inside_cols[None, None, :, None]
     conv_input = pad_rows(jnp.where(inside, normed, jnp.zeros_like(normed)))
-    full_weight = lax.all_gather(conv_weight, "section", axis=1, tiled=True)
+
+    def prepare_sheets_for(array_here, out_dim):
+        shares = lax.psum(1, axis_name="section")
+        f_now = sorted(((tick, (tick + 1) % shares) for tick in range(shares)))
+        seen_now = array_here
+        lanes = [seen_now]
+        for h in range(1, shares):
+            seen_now = lax.ppermute(seen_now, axis_name="section", perm=f_now)
+            lanes.insert(0, seen_now)
+        value_now = jnp.concatenate(lanes, axis=out_dim)
+        step_out = lax.axis_index("section") + 1
+        extra = jnp.roll(value_now, step_out * array_here.shape[out_dim], axis=out_dim)
+        return extra
+
+    full_weight = prepare_sheets_for(conv_weight, 1)
     mixed = conv_taps(conv_input, full_weight, frames, height, columns)
     decoded = (
         upblock_half.astype(jnp.float32).reshape(-1, half_channels) + mixed + conv_bias

time: 159 us -> 190 us (1.19)
  local copies, waits for them, and re-layouts: 30.1 us -> 51.6 us
  between operations: 14.7 us -> 1.44 us
  waiting for transfers between devices: 70.6 us -> 79.8 us
  other arithmetic: 16.3 us -> 24.9 us
  starting transfers between devices: 12 us -> 15.1 us
  matrix products: 5.53 us -> 7.47 us
    all_gather x1 -> x0, waiting for transfers between devices: 55.2 us -> none  [shards(): full_weight = lax.all_gather(conv_weight, 'section', axis=1, tiled=True)]
    ppermute x0 -> x3, waiting for transfers between devices: none -> 47.8 us  [prepare_sheets_for(): seen_now = lax.ppermute(seen_now, axis_name='section', perm=f_now)]
    all_to_all x1, waiting for transfers between devices: 7.51 us -> 25.1 us  [shards(): lax.all_to_all(outgoing, 'section', split_axis=1, concat_axis=0, tiled=True)]
    reshape x18, local copies, waits for them, and re-layouts: 10.7 us -> 24.4 us  [conv_taps(): window.reshape(-1, 3 * channels)]
    unnamed x78 -> x87, local copies, waits for them, and re-layouts: 3.68 us -> 12.4 us
    concatenate x14, other arithmetic: 14.1 us -> 20.7 us  [conv_taps(): jnp.concatenate([slab[:, :, 0:columns], slab[:, :, 1:columns + 1], slab[:...]
    ppermute x0 -> x3, starting transfers between devices: none -> 4.04 us  [prepare_sheets_for(): seen_now = lax.ppermute(seen_now, axis_name='section', perm=f_now)]
    slice x2, local copies, waits for them, and re-layouts: 4.44 us -> 1.36 us  [conv_taps(): taps = weight[first:first + 3].reshape(3 * channels, weight.shape[2])]
  transfers between devices with their start and end apart: 5 -> 7, of which waited for: 5 -> 6; matrix products, arithmetic and copies ran while one was open for 26% -> 35% of each run, Pallas kernels for 0% -> 0%
where the time goes in v1:
time: 190 us; the launch traced here: 189 us
  waiting for transfers between devices  79.8 us (42%)
  local copies, waits for them, and re-layouts  51.6 us (27%)
  other arithmetic  24.9 us (13%)
  starting transfers between devices  15.1 us (8%)
  blocking collectives  8.25 us (4%)
  matrix products  7.47 us (4%)
    ppermute x3, waiting for transfers between devices, prepare_sheets_for(): seen_now = lax.ppermute(seen_now, axis_name='section', perm=f_now)  47.8 us
    all_to_all x1, waiting for transfers between devices, shards(): lax.all_to_all(outgoing, 'section', split_axis=1, concat_axis=0, tiled=True)  25.1 us
    reshape x18, local copies, waits for them, and re-layouts, conv_taps(): window.reshape(-1, 3 * channels)  24.4 us
    concatenate x14, other arithmetic, conv_taps(): jnp.concatenate([slab[:, :, 0:columns], slab[:, :, 1:columns + 1], slab[:...  20.7 us
    unnamed x87, local copies, waits for them, and re-layouts  12.4 us
    dot_general x18, matrix products, conv_taps(): jnp.dot(window.reshape(-1, 3 * channels), taps, preferred_element_type=jn...  6.13 us
    slice x4, local copies, waits for them, and re-layouts, conv_taps(): slab[:, :, 0:columns]  6.1 us
    ppermute x1, waiting for transfers between devices, padded_2(): after = lax.ppermute(leading, axis, down)  4.23 us
  transfers between devices with their start and end apart: 7, of which 6 were waited for; matrix products, arithmetic and copies ran while one was open for 35% of the time, Pallas kernels for 0%

profile of v1, /device:TPU:0, one launch (start us, length us, event | category | flops | bytes accessed | tf_op | source)
XLA Modules:
  0.0 188.6 jit_solution(10033006741236151485)
XLA Ops:
  0.0 3.1 %collective-permute-start.3 = (bf16[27,128,256]{2,1,0:T(8,128)(2,1)}, bf16[27,128,256]{2,1,0:T(8,128)(2,1)S(1)}, u32[]{:S(2)}, u32[]{:S(2)}) collective-permute-start(bf16[27,128,256]{2,1,0:T(8,128)(2,1)} %param.26), channel_id=1, source_target_pairs={{0,4},{4,8},{8,12},{12,0},{1,5},{5,9},{9,13},{13,1},{2,6},{6,10},{... | collective-permute-start | bytes 5308424 | tf_op jit(solution)/shard_map/ppermute | solution.py:124
  3.1 1.2 convert_reduce_fusion
  5.2 2.5 %all-reduce.2 = (f32[64]{0:T(128)S(1)}, f32[64]{0:T(128)S(1)}) all-reduce(f32[64]{0:T(128)S(1)} %get-tuple-element.6, f32[64]{0:T(128)S(1)} %get-tuple-element.5), channel_id=1, replica_groups=mesh['groups'=2,'section'=4,'tp'=2,'sp'=2] {'tp'}, use_global_device_ids=true, to_apply=%region_3.0 | all-reduce | flops 128 | bytes 1024 | tf_op jit(solution)/shard_map/psum | solution.py:76
  8.4 1.3 fusion.19
  9.7 3.4 %psum.23 = f32[64,64]{1,0:T(8,128)S(1)} all-reduce(f32[64,64]{1,0:T(8,128)S(1)} %fusion.19), channel_id=1, replica_groups=mesh['groups'=2,'section'=4,'tp'=2,'sp'=2] {'tp'}, use_global_device_ids=true, to_apply=%region_4.0 | all-reduce | flops 4096 | bytes 32768 | tf_op jit(solution)/shard_map/psum | solution.py:88
  13.9 3.9 %all-to-all-start = ((bf16[8,4,128]{2,0,1:T(8,128)(2,1)}), bf16[8,4,128]{2,0,1:T(8,128)(2,1)S(1)}, u32[]{:S(2)}, u32[]{:S(2)}) async-start(bf16[8,4,128]{2,0,1:T(8,128)(2,1)} %copy.17), calls=%async_computation | async-start | bytes 16384 | tf_op jit(solution)/shard_map/all_to_all | solution.py:91
  19.1 25.1 %all-to-all-done = bf16[8,4,128]{2,0,1:T(8,128)(2,1)S(1)} async-done(((bf16[8,4,128]{2,0,1:T(8,128)(2,1)}), bf16[8,4,128]{2,0,1:T(8,128)(2,1)S(1)}, u32[]{:S(2)}, u32[]{:S(2)}) %all-to-all-start) | async-done | bytes 8224 | tf_op jit(solution)/shard_map/all_to_all | solution.py:91
  44.6 2.5 %collective-permute-start = (bf16[4,16,2,16]{3,2,1,0:T(2,128)(2,1)S(1)}, bf16[4,16,2,16]{3,2,1,0:T(2,128)(2,1)S(1)}, u32[]{:S(2)}, u32[]{:S(2)}) collective-permute-start(bf16[4,16,2,16]{3,2,1,0:T(2,128)(2,1)S(1)} %get-tuple-element.81), channel_id=1, source_target_pairs={{0,4},{4,8},{8,12},{1,5},{5,9},{9,13},{2,6},{6,10},{10,14},{3,7},{... | collective-permute-start | bytes 12296 | tf_op jit(solution)/shard_map/ppermute | solution.py:16
  47.1 1.3 collective-permute-start.1
  48.6 4.2 %collective-permute-done.1 = bf16[4,16,2,16]{3,2,1,0:T(2,128)(2,1)S(1)} collective-permute-done((bf16[4,16,2,16]{3,2,1,0:T(2,128)(2,1)S(1)}, bf16[4,16,2,16]{3,2,1,0:T(2,128)(2,1)S(1)}, u32[]{:S(2)}, u32[]{:S(2)}) %collective-permute-start.1) | collective-permute-done | bytes 4128 | tf_op jit(solution)/shard_map/ppermute | solution.py:17
  53.0 3.4 %collective-permute-start.2 = (bf16[4,16,8,16]{3,2,1,0:T(8,128)(2,1)S(1)}, bf16[4,16,8,16]{3,2,1,0:T(8,128)(2,1)S(1)}, u32[]{:S(2)}, u32[]{:S(2)}) collective-permute-start(bf16[4,16,8,16]{3,2,1,0:T(8,128)(2,1)S(1)} %pad_maximum_fusion.18), channel_id=1, source_target_pairs={{0,1},{2,3},{4,5},{6,7},{8,9},{10,11},{12,13},{14,15},{16,17},{18,... | collective-permute-start | bytes 49160 | tf_op jit(solution)/shard_map/ppermute | solution.py:25
  56.5 2.4 %collective-permute-done.2 = bf16[4,16,8,16]{3,2,1,0:T(8,128)(2,1)S(1)} collective-permute-done((bf16[4,16,8,16]{3,2,1,0:T(8,128)(2,1)S(1)}, bf16[4,16,8,16]{3,2,1,0:T(8,128)(2,1)S(1)}, u32[]{:S(2)}, u32[]{:S(2)}) %collective-permute-start.2) | collective-permute-done | bytes 16416 | tf_op jit(solution)/shard_map/ppermute | solution.py:25
  59.1 1.1 pad_slice_fusion.1
  60.2 1.4 pad_slice_fusion.2
  62.6 1.2 pad_maximum_fusion.14
  63.8 1.7 reshape.208
  65.5 2.4 %pad_maximum_fusion.12 = (bf16[6,16,6,48]{3,2,1,0:T(8,128)(2,1)}, bf16[6,16,6,48]{3,2,1,0:T(8,128)(2,1)}) fusion(bf16[6,16,6,16]{3,2,1,0:T(8,128)(2,1)} %get-tuple-element.53, bf16[6,16,6,16]{3,2,1,0:T(8,128)(2,1)} %get-tuple-element.52, bf16[6,16,6,16]{3,2,1,0:T(8,128)(2,1)} %get-tuple-element.51, bf16[6,16,6,16]{3,2,1,0:T(8,128)(2,1)} %get-tuple-element.54, ...), kind=kLoop, calls=%fused_computation.58 | loop fusion | flops 331776 | bytes 221184 | tf_op jit(solution)/shard_map/concatenate | solution.py:34
  67.9 1.7 reshape.204
  69.6 2.4 %pad_maximum_fusion.10 = (bf16[6,16,6,48]{3,2,1,0:T(8,128)(2,1)S(1)}, bf16[6,16,6,48]{3,2,1,0:T(8,128)(2,1)}) fusion(bf16[6,16,6,16]{3,2,1,0:T(8,128)(2,1)} %get-tuple-element.68, bf16[6,16,6,16]{3,2,1,0:T(8,128)(2,1)} %get-tuple-element.69, bf16[6,16,6,16]{3,2,1,0:T(8,128)(2,1)} %get-tuple-element.70, bf16[6,16,6,16]{3,2,1,0:T(8,128)(2,1)S(1)} %get-tuple-element.65, ...), kind=kLoop, calls=%fused_computation.56 | loop fusion | flops 331776 | bytes 221184 | tf_op jit(solution)/shard_map/concatenate | solution.py:34
  72.7 1.2 pad_maximum_fusion.9
  73.9 1.7 reshape.198
  75.6 1.7 reshape.202
  80.7 1.2 fusion.30
  84.6 2.4 %all_gather.3 = bf16[6,16,6,512]{3,2,1,0:T(8,128)(2,1)S(1)} all-gather(bf16[6,16,6,256]{3,2,1,0:T(8,128)(2,1)S(1)} %reshape.216), channel_id=1, replica_groups=mesh['groups'=2,'section'=4,'tp'=2,'sp'=2] {'tp'}, dimensions={3}, use_global_device_ids=true | all-gather | bytes 884736 | tf_op jit(solution)/shard_map/all_gather | solution.py:108
  88.8 1.4 fusion.25
  90.1 1.2 pad_maximum_fusion.1
  91.4 1.6 reshape.221
  93.0 2.3 %pad_slice_fusion.20 = (bf16[4,16,4,512]{3,2,1,0:T(4,128)(2,1)}, bf16[4,16,4,512]{3,2,1,0:T(4,128)(2,1)S(1)}, bf16[4,16,4,512]{3,2,1,0:T(4,128)(2,1)S(1)}, bf16[...) fusion(bf16[6,16,6,512]{3,2,1,0:T(8,128)(2,1)S(1)} %fusion.18), kind=kLoop, calls=%fused_computation.113 | loop fusion | bytes 3670016 | tf_op jit(solution)/shard_map/slice | solution.py:35
  95.3 1.2 pad_maximum_fusion
  96.5 2.3 %reshape.219 = bf16[256,1536]{1,0:T(8,128)(2,1)} reshape(bf16[4,16,4,1536]{3,2,1,0:T(4,128)(2,1)} %pad_maximum_fusion) | data formatting | bytes 1572864 | tf_op jit(solution)/shard_map/reshape | solution.py:41
  98.8 2.3 %pad_maximum_fusion.2 = bf16[4,16,4,1536]{3,2,1,0:T(4,128)(2,1)} fusion(bf16[4,16,4,512]{3,2,1,0:T(4,128)(2,1)} %get-tuple-element.23, bf16[4,16,4,512]{3,2,1,0:T(4,128)(2,1)} %get-tuple-element.22, bf16[4,16,4,512]{3,2,1,0:T(4,128)(2,1)} %get-tuple-element.21), kind=kLoop, calls=%fused_computation.42 | loop fusion | flops 2359296 | bytes 1572864 | tf_op jit(solution)/shard_map/concatenate | solution.py:34
  101.1 2.3 %reshape.223 = bf16[256,1536]{1,0:T(8,128)(2,1)} reshape(bf16[4,16,4,1536]{3,2,1,0:T(4,128)(2,1)} %pad_maximum_fusion.2) | data formatting | bytes 1572864 | tf_op jit(solution)/shard_map/reshape | solution.py:41
  103.4 2.3 %pad_maximum_fusion.3 = bf16[4,16,4,1536]{3,2,1,0:T(4,128)(2,1)} fusion(bf16[4,16,4,512]{3,2,1,0:T(4,128)(2,1)} %get-tuple-element.26, bf16[4,16,4,512]{3,2,1,0:T(4,128)(2,1)} %get-tuple-element.25, bf16[4,16,4,512]{3,2,1,0:T(4,128)(2,1)} %get-tuple-element.24), kind=kLoop, calls=%fused_computation.43 | loop fusion | flops 2359296 | bytes 1572864 | tf_op jit(solution)/shard_map/concatenate | solution.py:34
  105.7 2.3 %reshape.225 = bf16[256,1536]{1,0:T(8,128)(2,1)} reshape(bf16[4,16,4,1536]{3,2,1,0:T(4,128)(2,1)} %pad_maximum_fusion.3) | data formatting | bytes 1572864 | tf_op jit(solution)/shard_map/reshape | solution.py:41
  108.0 22.0 %collective-permute-done.4 = bf16[27,128,256]{2,1,0:T(8,128)(2,1)} collective-permute-done((bf16[27,128,256]{2,1,0:T(8,128)(2,1)S(1)}, bf16[27,128,256]{2,1,0:T(8,128)(2,1)}, u32[]{:S(2)}, u32[]{:S(2)}) %collective-permute-start.4) | collective-permute-done | bytes 1769504 | tf_op jit(solution)/shard_map/ppermute | solution.py:124
  130.1 2.7 %pad_slice_fusion.19 = (bf16[4,16,4,512]{3,2,1,0:T(4,128)(2,1)}, bf16[4,16,4,512]{3,2,1,0:T(4,128)(2,1)}, bf16[4,16,4,512]{3,2,1,0:T(4,128)(2,1)}, bf16[4,16,4,5...) fusion(bf16[6,16,6,512]{3,2,1,0:T(8,128)(2,1)S(1)} %fusion.18), kind=kLoop, calls=%fused_computation.112 | loop fusion | bytes 4456448 | tf_op jit(solution)/shard_map/slice | solution.py:35
  134.2 1.4 pad_maximum_fusion.5
  136.8 1.4 pad_maximum_fusion.6
  138.2 1.1 reshape.231
  139.3 1.4 pad_maximum_fusion.7
  140.8 1.1 reshape.233
  141.9 1.4 pad_maximum_fusion.8
  146.2 25.8 %collective-permute-done.5 = bf16[27,128,256]{2,1,0:T(8,128)(2,1)} collective-permute-done((bf16[27,128,256]{2,1,0:T(8,128)(2,1)}, bf16[27,128,256]{2,1,0:T(8,128)(2,1)}, u32[]{:S(2)}, u32[]{:S(2)}) %collective-permute-start.5) | collective-permute-done | bytes 1769504 | tf_op jit(solution)/shard_map/ppermute | solution.py:124
  172.0 1.7 constant_dynamic-update-slice_fusion.7
  173.6 1.7 constant_dynamic-update-slice_fusion.6
  175.4 1.3 copy-done.2
  176.9 1.7 constant_dynamic-update-slice_fusion.3
  178.6 1.7 constant_dynamic-update-slice_fusion.2
  (139 shorter events, 27.2 us)
Async XLA Ops:
  0.0 8.4 %copy-start = (bf16[3072,64]{0,1:T(8,128)(2,1)S(1)}, bf16[3072,64]{0,1:T(8,128)(2,1)}, u32[]{:S(2)}) copy-start(bf16[3072,64]{0,1:T(8,128)(2,1)} %param.17) | copy-start | bytes 1179652
  0.0 13.2 %copy-start.37 = (f32[64]{0:T(128)S(1)}, f32[64]{0:T(128)}, u32[]{:S(2)}) copy-start(f32[64]{0:T(128)} %param.18) | copy-start | bytes 772
  0.0 17.7 %copy-start.23 = (bf16[27,16,256]{2,1,0:T(8,128)(2,1)S(1)}, bf16[27,16,256]{2,1,0:T(8,128)(2,1)}, u32[]{:S(2)}) copy-start(bf16[27,16,256]{2,1,0:T(8,128)(2,1)} %param.23) | copy-start | bytes 663556
  0.0 44.4 %copy-start.33 = (bf16[4,16,4,16]{3,2,1,0:T(4,128)(2,1)S(1)}, bf16[4,16,4,16]{3,2,1,0:T(4,128)(2,1)}, u32[]{:S(2)}) copy-start(bf16[4,16,4,16]{3,2,1,0:T(4,128)(2,1)} %param.19) | copy-start | bytes 24580
  0.0 44.4 %copy-start.38 = (f32[16]{0:T(128)S(1)}, f32[16]{0:T(128)}, u32[]{:S(2)}) copy-start(f32[16]{0:T(128)} %param.21) | copy-start | bytes 196
  0.0 44.4 %copy-start.39 = (f32[16]{0:T(128)S(1)}, f32[16]{0:T(128)}, u32[]{:S(2)}) copy-start(f32[16]{0:T(128)} %param.22) | copy-start | bytes 196
  0.0 87.2 %collective-permute-start.3 = (bf16[27,128,256]{2,1,0:T(8,128)(2,1)}, bf16[27,128,256]{2,1,0:T(8,128)(2,1)S(1)}, u32[]{:S(2)}, u32[]{:S(2)}) collective-permute-start(bf16[27,128,256]{2,1,0:T(8,128)(2,1)} %param.26), channel_id=1, source_target_pairs={{0,4},{4,8},{8,12},{12,0},{1,5},{5,9},{9,13},{13,1},{2,6},{6,10},{... | collective-permute-start | bytes 5308424 | tf_op jit(solution)/shard_map/ppermute | solution.py:124
  13.9 30.3 %all-to-all-start = ((bf16[8,4,128]{2,0,1:T(8,128)(2,1)}), bf16[8,4,128]{2,0,1:T(8,128)(2,1)S(1)}, u32[]{:S(2)}, u32[]{:S(2)}) async-start(bf16[8,4,128]{2,0,1:T(8,128)(2,1)} %copy.17), calls=%async_computation | async-start | bytes 16384 | tf_op jit(solution)/shard_map/all_to_all | solution.py:91
  44.6 4.1 %collective-permute-start = (bf16[4,16,2,16]{3,2,1,0:T(2,128)(2,1)S(1)}, bf16[4,16,2,16]{3,2,1,0:T(2,128)(2,1)S(1)}, u32[]{:S(2)}, u32[]{:S(2)}) collective-permute-start(bf16[4,16,2,16]{3,2,1,0:T(2,128)(2,1)S(1)} %get-tuple-element.81), channel_id=1, source_target_pairs={{0,4},{4,8},{8,12},{1,5},{5,9},{9,13},{2,6},{6,10},{10,14},{3,7},{... | collective-permute-start | bytes 12296 | tf_op jit(solution)/shard_map/ppermute | solution.py:16
  47.1 5.8 %collective-permute-start.1 = (bf16[4,16,2,16]{3,2,1,0:T(2,128)(2,1)S(1)}, bf16[4,16,2,16]{3,2,1,0:T(2,128)(2,1)S(1)}, u32[]{:S(2)}, u32[]{:S(2)}) collective-permute-start(bf16[4,16,2,16]{3,2,1,0:T(2,128)(2,1)S(1)} %get-tuple-element.82), channel_id=1, source_target_pairs={{4,0},{8,4},{12,8},{5,1},{9,5},{13,9},{6,2},{10,6},{14,10},{7,3},{... | collective-permute-start | bytes 12296 | tf_op jit(solution)/shard_map/ppermute | solution.py:17
  53.0 5.9 %collective-permute-start.2 = (bf16[4,16,8,16]{3,2,1,0:T(8,128)(2,1)S(1)}, bf16[4,16,8,16]{3,2,1,0:T(8,128)(2,1)S(1)}, u32[]{:S(2)}, u32[]{:S(2)}) collective-permute-start(bf16[4,16,8,16]{3,2,1,0:T(8,128)(2,1)S(1)} %pad_maximum_fusion.18), channel_id=1, source_target_pairs={{0,1},{2,3},{4,5},{6,7},{8,9},{10,11},{12,13},{14,15},{16,17},{18,... | collective-permute-start | bytes 49160 | tf_op jit(solution)/shard_map/ppermute | solution.py:25
  72.7 7.6 %copy-start.16 = (bf16[6,16,6,16]{3,2,1,0:T(8,128)(2,1)S(1)}, bf16[6,16,6,16]{3,2,1,0:T(8,128)(2,1)}, u32[]{:S(2)}) copy-start(bf16[6,16,6,16]{3,2,1,0:T(8,128)(2,1)} %get-tuple-element.55) | copy-start | bytes 55300
  72.7 7.6 %copy-start.17 = (bf16[6,16,6,16]{3,2,1,0:T(8,128)(2,1)S(1)}, bf16[6,16,6,16]{3,2,1,0:T(8,128)(2,1)}, u32[]{:S(2)}) copy-start(bf16[6,16,6,16]{3,2,1,0:T(8,128)(2,1)} %get-tuple-element.62) | copy-start | bytes 55300
  72.7 7.6 %copy-start.18 = (bf16[6,16,6,16]{3,2,1,0:T(8,128)(2,1)S(1)}, bf16[6,16,6,16]{3,2,1,0:T(8,128)(2,1)}, u32[]{:S(2)}) copy-start(bf16[6,16,6,16]{3,2,1,0:T(8,128)(2,1)} %get-tuple-element.45) | copy-start | bytes 55300
  73.9 6.8 %copy-start.24 = (bf16[3,16,256]{2,1,0:T(8,128)(2,1)S(1)}, bf16[3,16,256]{2,1,0:T(8,128)(2,1)}, u32[]{:S(2)}) copy-start(bf16[3,16,256]{2,1,0:T(8,128)(2,1)} %get-tuple-element.79) | copy-start | bytes 73732
  75.6 6.3 %copy-start.21 = (bf16[576,48]{1,0:T(8,128)(2,1)S(1)}, bf16[576,48]{1,0:T(8,128)(2,1)}, u32[]{:S(2)}) copy-start(bf16[576,48]{1,0:T(8,128)(2,1)} %reshape.200) | copy-start | bytes 165892
  75.6 6.3 %copy-start.32 = (bf16[3,16,256]{2,1,0:T(8,128)(2,1)S(1)}, bf16[3,16,256]{2,1,0:T(8,128)(2,1)}, u32[]{:S(2)}) copy-start(bf16[3,16,256]{2,1,0:T(8,128)(2,1)} %get-tuple-element.78) | copy-start | bytes 73732
  80.4 1.8 copy-start.31
  80.6 1.5 copy-start.22
  80.7 1.7 copy-start.20
  80.7 1.7 copy-start.30
  82.1 0.7 copy-start.29
  82.4 0.9 copy-start.19
  82.4 0.9 copy-start.28
  82.6 0.9 copy-start.27
  83.1 0.8 copy-start.26
  83.5 0.7 copy-start.25
  83.5 0.7 copy-start.35
  84.5 3.7 %copy-start.34 = (f32[512]{0:T(512)S(1)}, f32[512]{0:T(512)}, u32[]{:S(2)}) copy-start(f32[512]{0:T(512)} %param.25) | copy-start | bytes 6148
  84.6 2.7 %copy-start.11 = (bf16[6,16,6,256]{3,2,1,0:T(8,128)(2,1)}, bf16[6,16,6,256]{3,2,1,0:T(8,128)(2,1)S(1)}, u32[]{:S(2)}) copy-start(bf16[6,16,6,256]{3,2,1,0:T(8,128)(2,1)S(1)} %reshape.216) | copy-start | bytes 884740
  87.3 42.8 %collective-permute-start.4 = (bf16[27,128,256]{2,1,0:T(8,128)(2,1)S(1)}, bf16[27,128,256]{2,1,0:T(8,128)(2,1)}, u32[]{:S(2)}, u32[]{:S(2)}) collective-permute-start(bf16[27,128,256]{2,1,0:T(8,128)(2,1)S(1)} %collective-permute-done.3), channel_id=1, source_target_pairs={{0,4},{4,8},{8,12},{12,0},{1,5},{5,9},{9,13},{13,1},{2,6},{6,10},{... | collective-permute-start | bytes 5308424 | tf_op jit(solution)/shard_map/ppermute | solution.py:124
  92.9 2.3 %copy-start.14 = (bf16[4,16,4,512]{3,2,1,0:T(4,128)(2,1)S(1)}, bf16[4,16,4,512]{3,2,1,0:T(4,128)(2,1)}, u32[]{:S(2)}) copy-start(bf16[4,16,4,512]{3,2,1,0:T(4,128)(2,1)} %get-tuple-element.44) | copy-start | bytes 786436
  108.0 24.8 %copy-start.12 = (bf16[4,16,4,512]{3,2,1,0:T(4,128)(2,1)S(1)}, bf16[4,16,4,512]{3,2,1,0:T(4,128)(2,1)}, u32[]{:S(2)}) copy-start(bf16[4,16,4,512]{3,2,1,0:T(4,128)(2,1)} %get-tuple-element.39) | copy-start | bytes 786436
  108.0 24.8 %copy-start.13 = (bf16[4,16,4,512]{3,2,1,0:T(4,128)(2,1)S(1)}, bf16[4,16,4,512]{3,2,1,0:T(4,128)(2,1)}, u32[]{:S(2)}) copy-start(bf16[4,16,4,512]{3,2,1,0:T(4,128)(2,1)} %get-tuple-element.40) | copy-start | bytes 786436
  130.1 41.9 %collective-permute-start.5 = (bf16[27,128,256]{2,1,0:T(8,128)(2,1)}, bf16[27,128,256]{2,1,0:T(8,128)(2,1)}, u32[]{:S(2)}, u32[]{:S(2)}) collective-permute-start(bf16[27,128,256]{2,1,0:T(8,128)(2,1)} %collective-permute-done.4), channel_id=1, source_target_pairs={{0,4},{4,8},{8,12},{12,0},{1,5},{5,9},{9,13},{13,1},{2,6},{6,10},{... | collective-permute-start | bytes 5308424 | tf_op jit(solution)/shard_map/ppermute | solution.py:124
  175.3 1.5 copy-start.2
  181.2 1.1 copy-start.3
  181.2 1.5 copy-start.4
  182.7 1.1 copy-start.5
  183.1 1.2 copy-start.6
  184.2 1.2 copy-start.7
  184.7 1.2 copy-start.8
  185.7 1.2 copy-start.9
  186.2 1.2 copy-start.10
  186.3 1.2 copy-start.15
  186.3 1.2 copy-start.36
  186.9 1.7 copy-start.1
